TPU v7x, 256 devices: a whole 4x4x8 slice. The times are simulated.
256 devices in a mesh: rounds: 8 (over z), tiles: 32 (over y, x, core).
Axes of the slice: x: 4, y: 4, z: 8, core: 2. Of those that a mesh axis runs over, the one named last changes fastest.
Arguments:
- syndromes: int32 [8, 2, 8, 64, 64], P(None, None, 'rounds', 'tiles'), may hold values 0 or 1
- labels: int32 [2, 8], P(None, 'rounds'), may hold values from 0 to 1
- stab_gate: bfloat16 [64, 64, 512], P('tiles'), may hold values from -6 to 6
- bit_gate: float32 [512], replicated, may hold values from -6 to 6
- forget_bias: float32 [128], replicated, may hold values from -1 to 4
- conv_weight: bfloat16 [3, 3, 128, 512], replicated, may hold values from -0.375 to 0.375
- query: float32 [128], replicated, may hold values from -12 to 12
- readout_weight: float32 [128], replicated, may hold values from -6 to 6
Outputs:
- grad_conv: float32 [3, 3, 128, 512], replicated
- grad_stab: float32 [64, 64, 512], P('tiles')
- grad_bit: float32 [512], replicated
- grad_forget: float32 [128], replicated
- grad_query: float32 [128], replicated
- grad_readout: float32 [128], replicated
- loss: float32 [], replicated
All inputs are finite; a program needn't handle non-finite values. No bound on the sum of `syndromes` on one device may be relied on, other than what follows from the above.
Results may differ from a plain program's by a relative error of at most 0.014.
Values may be sent and summed in bfloat16 or wider, within the bound.
No kernel may reach another device: no remote copies, remote signals or barrier semaphores. Data moves between devices by JAX's collectives and lax.ppermute only.
A program may use at most 64 MiB of HBM per device.

v0:
```python
import math
import jax
import jax.numpy as jnp
from jax import lax
from jax.sharding import PartitionSpec as P


def with_halo(cells, sides, width):
    for axis, dim in sides:
        count = lax.axis_size(axis)
        ends = count - 1
        head = lax.slice_in_dim(cells, 0, width, axis=dim)
        tail = lax.slice_in_dim(cells, cells.shape[dim] - width, cells.shape[dim], axis=dim)
        cells = jnp.concatenate(
            [
                lax.ppermute(tail, axis, [(i, (i + 1) % count) for i in range(ends)]),
                cells,
                lax.ppermute(head, axis, [((i + 1) % count, i) for i in range(ends)]),
            ],
            axis=dim,
        )
    return cells


def make_patches(padded):
    row_count = padded.shape[1] - 2
    col_count = padded.shape[2] - 2
    pieces = [
        padded[:, a : a + row_count, b : b + col_count, :] for a in range(3) for b in range(3)
    ]
    return jnp.concatenate(pieces, axis=-1).reshape(-1, 9 * padded.shape[3])


def pad_columns(d_field):
    return jnp.pad(d_field, ((0, 0), (0, 0), (1, 1), (0, 0)))


def cell_forward(gate_input, cell_prev, channels):
    input_gate = jax.nn.sigmoid(gate_input[:, :channels])
    forget = jax.nn.sigmoid(gate_input[:, channels : 2 * channels])
    candidate = jnp.tanh(gate_input[:, 2 * channels : 3 * channels])
    output_gate = jax.nn.sigmoid(gate_input[:, 3 * channels :])
    cell_new = forget * cell_prev + input_gate * candidate
    hidden_new = (output_gate * jnp.tanh(cell_new)).astype(jnp.bfloat16)
    gate_values = jnp.concatenate([input_gate, forget, candidate, output_gate], axis=1)
    return (gate_values, cell_new, hidden_new)


def cell_backward(gate_values, cell_prev, cell_new, d_hidden, d_cell, channels):
    input_gate = gate_values[:, :channels]
    forget = gate_values[:, channels : 2 * channels]
    candidate = gate_values[:, 2 * channels : 3 * channels]
    output_gate = gate_values[:, 3 * channels :]
    squash = jnp.tanh(cell_new)
    d_total = d_cell + d_hidden * output_gate * (1.0 - squash * squash)
    d_gates = jnp.concatenate(
        [
            d_total * candidate * input_gate * (1.0 - input_gate),
            d_total * cell_prev * forget * (1.0 - forget),
            d_total * input_gate * (1.0 - candidate * candidate),
            d_hidden * squash * output_gate * (1.0 - output_gate),
        ],
        axis=1,
    ).astype(jnp.bfloat16)
    return (d_gates, d_total * forget)


def column_total(products, col_count, row_shift):
    result = products[:, :, 2 : 2 + col_count, row_shift, 0]
    for col_shift in range(1, 3):
        result = (
            result + products[:, :, 2 - col_shift : 2 - col_shift + col_count, row_shift, col_shift]
        )
    return result


def transpose_products(d_field, weight_matrix, channels):
    products = lax.dot_general(
        d_field, weight_matrix, (((3,), (1,)), ((), ())), preferred_element_type=jnp.float32
    )
    return products.reshape(d_field.shape[:3] + (3, 3, channels))


def per_device(
    syndromes, labels, stab_gate, bit_gate, forget_bias, conv_weight, query, readout_weight
):
    round_count, micro_count, shot_count, tile_rows, columns = syndromes.shape
    channels = conv_weight.shape[2]
    gate_units = conv_weight.shape[3]
    tile_sites = tile_rows * columns
    flat_rows = shot_count * tile_sites
    weight_matrix = conv_weight.reshape(9 * channels, gate_units)
    stab_rows = stab_gate.reshape(1, tile_sites, gate_units).astype(jnp.float32)
    forget_shift = jnp.concatenate(
        [jnp.zeros((channels,), jnp.float32), forget_bias, jnp.zeros((2 * channels,), jnp.float32)]
    )
    score_scale = 1.0 / math.sqrt(channels)
    field_shape = (shot_count, tile_rows, columns, channels)
    gate_shape = (shot_count, tile_rows, columns, gate_units)
    lead_tile = (lax.axis_index("tiles") == 0).astype(jnp.float32)

    def forward_round(recurrent, fired_bits):
        hidden_prev, cell_prev = recurrent
        hidden_rows = with_halo(hidden_prev, (("tiles", 1),), 1)
        hidden_pad = pad_columns(hidden_rows)
        gate_input = jnp.dot(
            make_patches(hidden_pad), weight_matrix, preferred_element_type=jnp.float32
        )
        gate_input = (
            gate_input.reshape(shot_count, tile_sites, gate_units)
            + stab_rows
            + fired_bits.astype(jnp.float32).reshape(shot_count, tile_sites, 1) * bit_gate
            + forget_shift
        )
        gate_values, cell_new, hidden_new = cell_forward(
            gate_input.reshape(flat_rows, gate_units), cell_prev, channels
        )
        return (
            (hidden_new.reshape(field_shape), cell_new),
            (hidden_pad, gate_values, cell_prev, cell_new, fired_bits),
        )

    def backward_round(state_carry, saved_items):
        d_hidden, d_cell, grad_weight, grad_stab_part, grad_fired, grad_keep = state_carry
        hidden_pad, gate_values, cell_prev, cell_new, fired_bits = saved_items
        d_gates, d_cell_prev = cell_backward(
            gate_values, cell_prev, cell_new, d_hidden, d_cell, channels
        )
        grad_weight = grad_weight + lax.dot_general(
            make_patches(hidden_pad),
            d_gates,
            (((0,), (0,)), ((), ())),
            preferred_element_type=jnp.float32,
        )
        grad_stab_part = grad_stab_part + jnp.sum(
            d_gates.reshape(shot_count, tile_sites, gate_units).astype(jnp.float32), axis=0
        )
        fired_row = fired_bits.astype(jnp.bfloat16).reshape(1, flat_rows)
        grad_fired = grad_fired + jnp.dot(fired_row, d_gates, preferred_element_type=jnp.float32)[0]
        grad_keep = grad_keep + jnp.sum(
            d_gates[:, channels : 2 * channels].astype(jnp.float32), axis=0
        )
        d_field = d_gates.reshape(gate_shape)
        d_rows = with_halo(d_field, (("tiles", 1),), 1)
        products = transpose_products(pad_columns(d_rows), weight_matrix, channels)
        d_hidden_prev = column_total(products[:, 2 : 2 + tile_rows], columns, 0)
        for row_shift in range(1, 3):
            d_hidden_prev = d_hidden_prev + column_total(
                products[:, 2 - row_shift : 2 - row_shift + tile_rows], columns, row_shift
            )
        return (
            (
                d_hidden_prev.reshape(flat_rows, channels),
                d_cell_prev,
                grad_weight,
                grad_stab_part,
                grad_fired,
                grad_keep,
            ),
            None,
        )

    def one_batch(totals, inputs):
        fired_rounds, batch_labels = inputs
        initial = (
            jnp.zeros(field_shape, jnp.bfloat16),
            jnp.zeros((flat_rows, channels), jnp.float32),
        )
        (hidden_last, unused_cell), saved = lax.scan(forward_round, initial, fired_rounds)
        hidden_full = hidden_last.astype(jnp.float32).reshape(shot_count, tile_sites, channels)
        scores = jnp.sum(hidden_full * query, axis=2) * score_scale
        exp_score = jnp.exp(scores)
        part_total = jnp.sum(exp_score, axis=1)
        part_numer = jnp.sum(exp_score[..., None] * hidden_full, axis=1)
        total_exp, numer = lax.psum((part_total, part_numer), "tiles")
        pooled = numer / total_exp[:, None]
        logit_value = jnp.sum(pooled * readout_weight, axis=1)
        targets = batch_labels.astype(jnp.float32)
        loss_part = jnp.sum(jax.nn.softplus(logit_value) - targets * logit_value)
        d_logit = jax.nn.sigmoid(logit_value) - targets
        d_pooled = d_logit[:, None] * readout_weight
        weight = exp_score / total_exp[:, None]
        d_score = weight * (
            jnp.sum(hidden_full * d_pooled[:, None, :], axis=2)
            - jnp.sum(pooled * d_pooled, axis=1)[:, None]
        )
        final_grad = (
            weight[..., None] * d_pooled[:, None, :] + d_score[..., None] * query * score_scale
        )
        query_part = score_scale * jnp.sum(d_score[..., None] * hidden_full, axis=(0, 1))
        readout_part = jnp.sum(d_logit[:, None] * pooled, axis=0)
        grad_weight, grad_stab_part, grad_fired, grad_keep, grad_query, grad_readout, loss_total = (
            totals
        )
        start_back = (
            final_grad.reshape(flat_rows, channels),
            jnp.zeros((flat_rows, channels), jnp.float32),
            grad_weight,
            grad_stab_part,
            grad_fired,
            grad_keep,
        )
        back_state, unused_out = lax.scan(backward_round, start_back, saved, reverse=True)
        return (
            (
                back_state[2],
                back_state[3],
                back_state[4],
                back_state[5],
                grad_query + query_part,
                grad_readout + readout_part,
                loss_total + loss_part,
            ),
            None,
        )

    zero_totals = (
        jnp.zeros((9 * channels, gate_units), jnp.float32),
        jnp.zeros((tile_sites, gate_units), jnp.float32),
        jnp.zeros((gate_units,), jnp.float32),
        jnp.zeros((channels,), jnp.float32),
        jnp.zeros((channels,), jnp.float32),
        jnp.zeros((channels,), jnp.float32),
        jnp.zeros((), jnp.float32),
    )
    batch_inputs = (jnp.swapaxes(syndromes, 0, 1), labels)
    sums, unused_out = lax.scan(one_batch, zero_totals, batch_inputs)
    grad_weight, grad_stab_part, grad_fired, grad_keep, grad_query, grad_readout, loss_total = sums
    stab_total = lax.psum(grad_stab_part.astype(jnp.bfloat16), "rounds").astype(jnp.float32)
    totals = lax.psum(
        (
            grad_weight,
            grad_fired,
            grad_keep,
            grad_query,
            grad_readout * lead_tile,
            loss_total * lead_tile,
        ),
        ("rounds", "tiles"),
    )
    return (
        totals[0].reshape(3, 3, channels, gate_units),
        stab_total.reshape(tile_rows, columns, gate_units),
        totals[1],
        totals[2],
        totals[3],
        totals[4],
        totals[5],
    )


def solution(mesh):
    in_specs = (
        P(None, None, "rounds", "tiles", None),
        P(None, "rounds"),
        P("tiles", None, None),
        P(),
        P(),
        P(),
        P(),
        P(),
    )
    out_specs = (P(), P("tiles", None, None), P(), P(), P(), P(), P())
    return jax.shard_map(
        per_device, mesh=mesh, in_specs=in_specs, out_specs=out_specs, check_vma=False
    )
```

profile of v0, /device:TPU:2, one launch (start us, length us, event | category | flops | bytes accessed | tf_op | source)
XLA Modules:
  0.0 1043.6 jit_solution(17618227137616668080)
XLA Ops:
  11.9 661.5 %while.108 = (s32[]{:T(128)}, f32[1152,512]{1,0:T(8,128)S(1)}, f32[128,512]{1,0:T(8,128)}, f32[512]{0:T(512)S(1)}, f32[128]{0:T(128)}, /*index=5*/f32[128]{0:T(1...) while((s32[]{:T(128)}, f32[1152,512]{1,0:T(8,128)S(1)}, ...), condition=%wide.region_15.16_spmd.clone, body=%wide.region_0.15_spmd.clone.sunk | while | flops 621755008 | bytes 24381452 | solution.py:227
  13.2 88.8 %while.109 = (s32[]{:T(128)}, bf16[1,2,64,128]{3,2,1,0:T(8,128)(2,1)S(1)}, f32[128,128]{1,0:T(8,128)S(1)}, bf16[8,1,4,66,128]{4,3,2,1,0:T(8,128)(2,1)}, f32[8,12...) while((s32[]{:T(128)}, ...), condition=%wide.region_2.2_spmd.clone, body=%wide.region_1.1_spmd.clone.sunk | while | flops 152739968 | bytes 4702967 | solution.py:169
  15.2 2.4 collective-permute-start.1
  18.4 2.5 collective-permute-done.1
  26.8 2.4 collective-permute-start.1
  37.8 2.4 collective-permute-start.1
  48.8 2.4 collective-permute-start.1
  59.9 2.4 collective-permute-start.1
  70.9 2.4 collective-permute-start.1
  81.9 2.4 collective-permute-start.1
  92.9 2.4 collective-permute-start.1
  103.6 68.7 %all-reduce.5 = (f32[]{:T(128)}, f32[1,128]{1,0:T(1,128)S(1)}) all-reduce(f32[]{:T(128)} %get-tuple-element.1439, f32[1,128]{1,0:T(1,128)S(1)} %bitcast.186), channel_id=1, replica_groups=mesh['rounds'=8,'tiles'=32] {'tiles'}, use_global_device_ids=true, to_apply=%region_5.5 | all-reduce | flops 129 | bytes 1032 | tf_op jit(solution)/shard_map/while/body/eval_jaxpr/psum | solution.py:175
  185.9 148.6 %while.110 = (s32[]{:T(128)}, f32[128,128]{1,0:T(8,128)S(1)}, f32[128,128]{1,0:T(8,128)}, f32[1152,512]{1,0:T(8,128)S(1)}, f32[128,512]{1,0:T(8,128)}, /*index=5...) while((s32[]{:T(128)}, f32[128,128]{1,0:T(8,128)S(1)}, ...), condition=%wide.region_13.13_spmd.clone, body=%wide.region_11.12_spmd.clone.sunk | while | flops 468750976 | bytes 19420224 | solution.py:203
  189.8 6.0 collective-permute-start.2
  195.8 1.9 collective-permute-start.3
  210.5 3.6 collective-permute-start.2
  228.7 3.6 collective-permute-start.2
  232.4 1.9 collective-permute-start.3
  247.1 3.6 collective-permute-start.2
  250.7 1.9 collective-permute-start.3
  265.3 3.6 collective-permute-start.2
  269.0 1.9 collective-permute-start.3
  283.6 3.6 collective-permute-start.2
  301.9 3.6 collective-permute-start.2
  320.1 3.6 collective-permute-start.2
  335.8 100.8 %while.109 = (s32[]{:T(128)}, bf16[1,2,64,128]{3,2,1,0:T(8,128)(2,1)S(1)}, f32[128,128]{1,0:T(8,128)S(1)}, bf16[8,1,4,66,128]{4,3,2,1,0:T(8,128)(2,1)}, f32[8,12...) while((s32[]{:T(128)}, ...), condition=%wide.region_2.2_spmd.clone, body=%wide.region_1.1_spmd.clone.sunk | while | flops 152739968 | bytes 4702967 | solution.py:169
  335.9 3.6 collective-permute-start
  339.5 3.2 collective-permute-start.1
  350.5 4.8 collective-permute-start.1
  362.1 5.8 collective-permute-start.1
  374.6 5.8 collective-permute-start.1
  387.2 5.8 collective-permute-start.1
  399.7 5.8 collective-permute-start.1
  412.3 6.3 collective-permute-start.1
  425.4 6.3 collective-permute-start.1
  438.3 72.4 %all-reduce.5 = (f32[]{:T(128)}, f32[1,128]{1,0:T(1,128)S(1)}) all-reduce(f32[]{:T(128)} %get-tuple-element.1439, f32[1,128]{1,0:T(1,128)S(1)} %bitcast.186), channel_id=1, replica_groups=mesh['rounds'=8,'tiles'=32] {'tiles'}, use_global_device_ids=true, to_apply=%region_5.5 | all-reduce | flops 129 | bytes 1032 | tf_op jit(solution)/shard_map/while/body/eval_jaxpr/psum | solution.py:175
  524.8 148.6 %while.110 = (s32[]{:T(128)}, f32[128,128]{1,0:T(8,128)S(1)}, f32[128,128]{1,0:T(8,128)}, f32[1152,512]{1,0:T(8,128)S(1)}, f32[128,512]{1,0:T(8,128)}, /*index=5...) while((s32[]{:T(128)}, f32[128,128]{1,0:T(8,128)S(1)}, ...), condition=%wide.region_13.13_spmd.clone, body=%wide.region_11.12_spmd.clone.sunk | while | flops 468750976 | bytes 19420224 | solution.py:203
  528.7 6.0 collective-permute-start.2
  549.4 3.6 collective-permute-start.2
  567.6 3.6 collective-permute-start.2
  585.9 3.6 collective-permute-start.2
  604.2 3.6 collective-permute-start.2
  622.5 3.6 collective-permute-start.2
  640.8 3.6 collective-permute-start.2
  659.0 3.6 collective-permute-start.2
  676.7 94.3 %all-reduce.3 = (f32[512]{0:T(512)}, f32[128]{0:T(128)}, f32[128]{0:T(128)}, f32[128]{0:T(128)}, f32[]{:T(128)}) all-reduce(f32[512]{0:T(512)S(1)} %get-tuple-element.1688, f32[128]{0:T(128)S(1)} %copy-done.13, f32[128]{0:T(128)} %get-tuple-element.1690, ...), channel_id=1, replica_groups=mesh['rounds'=8,'tiles'=32] {'rounds','tiles'}, use_global_device_ids=true, to_apply=%region_18.19 | all-reduce | flops 897 | bytes 7176 | tf_op jit(solution)/shard_map/psum | solution.py:230
  772.7 260.7 %all-reduce.9.cloned.1.call-done = f32[3,3,128,512]{3,2,1,0:T(8,128)} async-done(((f32[3,3,128,512]{3,2,1,0:T(8,128)}), f32[3,3,128,512]{3,2,1,0:T(8,128)}) %all-reduce.9.cloned.1.call-update) | async-done | bytes 2359312 | tf_op jit(solution)/shard_map/psum | solution.py:230
  1033.5 3.3 copy.108
  (1186 shorter events, 375.0 us)
Async XLA Ops:
  7.2 763.9 %all-reduce.11.cloned.1.call-start = ((), (), s32[]{:S(2)}) async-start(), calls=%async_computation.1 | async-start | bytes 262144 | tf_op jit(solution)/shard_map/psum | solution.py:229
  189.8 15.2 %collective-permute-start.2 = (bf16[1,1,64,512]{3,2,1,0:T(8,128)(2,1)}, bf16[1,1,64,512]{3,2,1,0:T(8,128)(2,1)}, u32[]{:S(2)}, u32[]{:S(2)}) collective-permute-start(bf16[1,1,64,512]{3,2,1,0:T(8,128)(2,1)} %get-tuple-element.1494), channel_id=1, source_target_pairs={{1,0},{2,1},{3,2},{4,3},{5,4},{6,5},{7,6},{8,7},{9,8},{10,9},{11,1... | collective-permute-start | bytes 196616 | tf_op jit(solution)/shard_map/while/body/eval_jaxpr/while/body/eval_jaxpr/ppermute | solution.py:18
  195.8 9.2 collective-permute-start.3
  210.5 12.8 %collective-permute-start.2 = (bf16[1,1,64,512]{3,2,1,0:T(8,128)(2,1)}, bf16[1,1,64,512]{3,2,1,0:T(8,128)(2,1)}, u32[]{:S(2)}, u32[]{:S(2)}) collective-permute-start(bf16[1,1,64,512]{3,2,1,0:T(8,128)(2,1)} %get-tuple-element.1494), channel_id=1, source_target_pairs={{1,0},{2,1},{3,2},{4,3},{5,4},{6,5},{7,6},{8,7},{9,8},{10,9},{11,1... | collective-permute-start | bytes 196616 | tf_op jit(solution)/shard_map/while/body/eval_jaxpr/while/body/eval_jaxpr/ppermute | solution.py:18
  214.1 9.2 collective-permute-start.3
  228.7 12.9 %collective-permute-start.2 = (bf16[1,1,64,512]{3,2,1,0:T(8,128)(2,1)}, bf16[1,1,64,512]{3,2,1,0:T(8,128)(2,1)}, u32[]{:S(2)}, u32[]{:S(2)}) collective-permute-start(bf16[1,1,64,512]{3,2,1,0:T(8,128)(2,1)} %get-tuple-element.1494), channel_id=1, source_target_pairs={{1,0},{2,1},{3,2},{4,3},{5,4},{6,5},{7,6},{8,7},{9,8},{10,9},{11,1... | collective-permute-start | bytes 196616 | tf_op jit(solution)/shard_map/while/body/eval_jaxpr/while/body/eval_jaxpr/ppermute | solution.py:18
  232.4 9.2 collective-permute-start.3
  247.1 12.8 %collective-permute-start.2 = (bf16[1,1,64,512]{3,2,1,0:T(8,128)(2,1)}, bf16[1,1,64,512]{3,2,1,0:T(8,128)(2,1)}, u32[]{:S(2)}, u32[]{:S(2)}) collective-permute-start(bf16[1,1,64,512]{3,2,1,0:T(8,128)(2,1)} %get-tuple-element.1494), channel_id=1, source_target_pairs={{1,0},{2,1},{3,2},{4,3},{5,4},{6,5},{7,6},{8,7},{9,8},{10,9},{11,1... | collective-permute-start | bytes 196616 | tf_op jit(solution)/shard_map/while/body/eval_jaxpr/while/body/eval_jaxpr/ppermute | solution.py:18
  250.7 9.2 collective-permute-start.3
  265.3 12.8 %collective-permute-start.2 = (bf16[1,1,64,512]{3,2,1,0:T(8,128)(2,1)}, bf16[1,1,64,512]{3,2,1,0:T(8,128)(2,1)}, u32[]{:S(2)}, u32[]{:S(2)}) collective-permute-start(bf16[1,1,64,512]{3,2,1,0:T(8,128)(2,1)} %get-tuple-element.1494), channel_id=1, source_target_pairs={{1,0},{2,1},{3,2},{4,3},{5,4},{6,5},{7,6},{8,7},{9,8},{10,9},{11,1... | collective-permute-start | bytes 196616 | tf_op jit(solution)/shard_map/while/body/eval_jaxpr/while/body/eval_jaxpr/ppermute | solution.py:18
  269.0 9.2 collective-permute-start.3
  283.6 12.8 %collective-permute-start.2 = (bf16[1,1,64,512]{3,2,1,0:T(8,128)(2,1)}, bf16[1,1,64,512]{3,2,1,0:T(8,128)(2,1)}, u32[]{:S(2)}, u32[]{:S(2)}) collective-permute-start(bf16[1,1,64,512]{3,2,1,0:T(8,128)(2,1)} %get-tuple-element.1494), channel_id=1, source_target_pairs={{1,0},{2,1},{3,2},{4,3},{5,4},{6,5},{7,6},{8,7},{9,8},{10,9},{11,1... | collective-permute-start | bytes 196616 | tf_op jit(solution)/shard_map/while/body/eval_jaxpr/while/body/eval_jaxpr/ppermute | solution.py:18
  287.2 9.2 collective-permute-start.3
  301.9 12.8 %collective-permute-start.2 = (bf16[1,1,64,512]{3,2,1,0:T(8,128)(2,1)}, bf16[1,1,64,512]{3,2,1,0:T(8,128)(2,1)}, u32[]{:S(2)}, u32[]{:S(2)}) collective-permute-start(bf16[1,1,64,512]{3,2,1,0:T(8,128)(2,1)} %get-tuple-element.1494), channel_id=1, source_target_pairs={{1,0},{2,1},{3,2},{4,3},{5,4},{6,5},{7,6},{8,7},{9,8},{10,9},{11,1... | collective-permute-start | bytes 196616 | tf_op jit(solution)/shard_map/while/body/eval_jaxpr/while/body/eval_jaxpr/ppermute | solution.py:18
  305.5 9.2 collective-permute-start.3
  320.1 12.8 %collective-permute-start.2 = (bf16[1,1,64,512]{3,2,1,0:T(8,128)(2,1)}, bf16[1,1,64,512]{3,2,1,0:T(8,128)(2,1)}, u32[]{:S(2)}, u32[]{:S(2)}) collective-permute-start(bf16[1,1,64,512]{3,2,1,0:T(8,128)(2,1)} %get-tuple-element.1494), channel_id=1, source_target_pairs={{1,0},{2,1},{3,2},{4,3},{5,4},{6,5},{7,6},{8,7},{9,8},{10,9},{11,1... | collective-permute-start | bytes 196616 | tf_op jit(solution)/shard_map/while/body/eval_jaxpr/while/body/eval_jaxpr/ppermute | solution.py:18
  323.8 9.2 collective-permute-start.3
  335.9 7.6 collective-permute-start
  348.6 7.4 collective-permute-start
  360.2 8.4 collective-permute-start
  362.1 6.6 collective-permute-start.1
  372.7 8.4 collective-permute-start
  374.6 6.6 collective-permute-start.1
  385.3 8.4 collective-permute-start
  387.2 6.6 collective-permute-start.1
  397.8 8.5 collective-permute-start
  399.7 6.6 collective-permute-start.1
  410.4 9.0 collective-permute-start
  412.3 7.2 collective-permute-start.1
  423.5 9.0 collective-permute-start
  425.4 7.2 collective-permute-start.1
  528.7 15.2 %collective-permute-start.2 = (bf16[1,1,64,512]{3,2,1,0:T(8,128)(2,1)}, bf16[1,1,64,512]{3,2,1,0:T(8,128)(2,1)}, u32[]{:S(2)}, u32[]{:S(2)}) collective-permute-start(bf16[1,1,64,512]{3,2,1,0:T(8,128)(2,1)} %get-tuple-element.1494), channel_id=1, source_target_pairs={{1,0},{2,1},{3,2},{4,3},{5,4},{6,5},{7,6},{8,7},{9,8},{10,9},{11,1... | collective-permute-start | bytes 196616 | tf_op jit(solution)/shard_map/while/body/eval_jaxpr/while/body/eval_jaxpr/ppermute | solution.py:18
  534.7 9.2 collective-permute-start.3
  549.4 12.8 %collective-permute-start.2 = (bf16[1,1,64,512]{3,2,1,0:T(8,128)(2,1)}, bf16[1,1,64,512]{3,2,1,0:T(8,128)(2,1)}, u32[]{:S(2)}, u32[]{:S(2)}) collective-permute-start(bf16[1,1,64,512]{3,2,1,0:T(8,128)(2,1)} %get-tuple-element.1494), channel_id=1, source_target_pairs={{1,0},{2,1},{3,2},{4,3},{5,4},{6,5},{7,6},{8,7},{9,8},{10,9},{11,1... | collective-permute-start | bytes 196616 | tf_op jit(solution)/shard_map/while/body/eval_jaxpr/while/body/eval_jaxpr/ppermute | solution.py:18
  553.0 9.2 collective-permute-start.3
  567.6 12.8 %collective-permute-start.2 = (bf16[1,1,64,512]{3,2,1,0:T(8,128)(2,1)}, bf16[1,1,64,512]{3,2,1,0:T(8,128)(2,1)}, u32[]{:S(2)}, u32[]{:S(2)}) collective-permute-start(bf16[1,1,64,512]{3,2,1,0:T(8,128)(2,1)} %get-tuple-element.1494), channel_id=1, source_target_pairs={{1,0},{2,1},{3,2},{4,3},{5,4},{6,5},{7,6},{8,7},{9,8},{10,9},{11,1... | collective-permute-start | bytes 196616 | tf_op jit(solution)/shard_map/while/body/eval_jaxpr/while/body/eval_jaxpr/ppermute | solution.py:18
  571.3 9.2 collective-permute-start.3
  585.9 12.8 %collective-permute-start.2 = (bf16[1,1,64,512]{3,2,1,0:T(8,128)(2,1)}, bf16[1,1,64,512]{3,2,1,0:T(8,128)(2,1)}, u32[]{:S(2)}, u32[]{:S(2)}) collective-permute-start(bf16[1,1,64,512]{3,2,1,0:T(8,128)(2,1)} %get-tuple-element.1494), channel_id=1, source_target_pairs={{1,0},{2,1},{3,2},{4,3},{5,4},{6,5},{7,6},{8,7},{9,8},{10,9},{11,1... | collective-permute-start | bytes 196616 | tf_op jit(solution)/shard_map/while/body/eval_jaxpr/while/body/eval_jaxpr/ppermute | solution.py:18
  589.6 9.2 collective-permute-start.3
  604.2 12.8 %collective-permute-start.2 = (bf16[1,1,64,512]{3,2,1,0:T(8,128)(2,1)}, bf16[1,1,64,512]{3,2,1,0:T(8,128)(2,1)}, u32[]{:S(2)}, u32[]{:S(2)}) collective-permute-start(bf16[1,1,64,512]{3,2,1,0:T(8,128)(2,1)} %get-tuple-element.1494), channel_id=1, source_target_pairs={{1,0},{2,1},{3,2},{4,3},{5,4},{6,5},{7,6},{8,7},{9,8},{10,9},{11,1... | collective-permute-start | bytes 196616 | tf_op jit(solution)/shard_map/while/body/eval_jaxpr/while/body/eval_jaxpr/ppermute | solution.py:18
  607.9 9.2 collective-permute-start.3
  622.5 12.8 %collective-permute-start.2 = (bf16[1,1,64,512]{3,2,1,0:T(8,128)(2,1)}, bf16[1,1,64,512]{3,2,1,0:T(8,128)(2,1)}, u32[]{:S(2)}, u32[]{:S(2)}) collective-permute-start(bf16[1,1,64,512]{3,2,1,0:T(8,128)(2,1)} %get-tuple-element.1494), channel_id=1, source_target_pairs={{1,0},{2,1},{3,2},{4,3},{5,4},{6,5},{7,6},{8,7},{9,8},{10,9},{11,1... | collective-permute-start | bytes 196616 | tf_op jit(solution)/shard_map/while/body/eval_jaxpr/while/body/eval_jaxpr/ppermute | solution.py:18
  626.1 9.2 collective-permute-start.3
  640.8 12.8 %collective-permute-start.2 = (bf16[1,1,64,512]{3,2,1,0:T(8,128)(2,1)}, bf16[1,1,64,512]{3,2,1,0:T(8,128)(2,1)}, u32[]{:S(2)}, u32[]{:S(2)}) collective-permute-start(bf16[1,1,64,512]{3,2,1,0:T(8,128)(2,1)} %get-tuple-element.1494), channel_id=1, source_target_pairs={{1,0},{2,1},{3,2},{4,3},{5,4},{6,5},{7,6},{8,7},{9,8},{10,9},{11,1... | collective-permute-start | bytes 196616 | tf_op jit(solution)/shard_map/while/body/eval_jaxpr/while/body/eval_jaxpr/ppermute | solution.py:18
  644.4 9.2 collective-permute-start.3
  659.0 12.8 %collective-permute-start.2 = (bf16[1,1,64,512]{3,2,1,0:T(8,128)(2,1)}, bf16[1,1,64,512]{3,2,1,0:T(8,128)(2,1)}, u32[]{:S(2)}, u32[]{:S(2)}) collective-permute-start(bf16[1,1,64,512]{3,2,1,0:T(8,128)(2,1)} %get-tuple-element.1494), channel_id=1, source_target_pairs={{1,0},{2,1},{3,2},{4,3},{5,4},{6,5},{7,6},{8,7},{9,8},{10,9},{11,1... | collective-permute-start | bytes 196616 | tf_op jit(solution)/shard_map/while/body/eval_jaxpr/while/body/eval_jaxpr/ppermute | solution.py:18
  662.7 9.2 collective-permute-start.3
  675.3 358.1 %all-reduce.9.cloned.1.call-start = ((), (), s32[]{:S(2)}) async-start(), calls=%async_computation | async-start | bytes 4718592 | tf_op jit(solution)/shard_map/psum | solution.py:230
  (198 other events, 933.2 us)
Sparse Core Ops, SparseCore 0:
  675.4 90.3 all-reduce.10
  771.8 261.6 all-reduce.8
where the time goes:
time: 1050 us; the launch traced here: 1040 us
  waiting for transfers between devices  279 us (27%)
  blocking collectives  235 us (22%)
  starting transfers between devices  189 us (18%)
  other arithmetic  168 us (16%)
  matrix products  77.6 us (7%)
  local copies, waits for them, and re-layouts  65.3 us (6%)
  loops' own time  15.4 us (1%)
  between operations  14.1 us (1%)
    psum x1, waiting for transfers between devices, per_device(): lax.psum((grad_weight, grad_fired, grad_keep, grad_query, grad_readout *...  261 us
    psum x2, blocking collectives, one_batch(): total_exp, numer = lax.psum((part_total, part_numer), 'tiles')  141 us
    ppermute x32, starting transfers between devices, with_halo(): lax.ppermute(head, axis, [((i + 1) % count, i) for i in range(ends)])  95.1 us
    psum x1, blocking collectives, per_device(): lax.psum((grad_weight, grad_fired, grad_keep, grad_query, grad_readout *...  94.3 us
    ppermute x32, starting transfers between devices, with_halo(): lax.ppermute(tail, axis, [(i, (i + 1) % count) for i in range(ends)])  93.7 us
    dynamic_update_slice x48, other arithmetic, one_batch(): lax.scan(forward_round, initial, fired_rounds)  33.1 us
    squeeze x32, local copies, waits for them, and re-layouts, one_batch(): lax.scan(backward_round, start_back, saved, reverse=True)  29.9 us
    add x16, other arithmetic, backward_round(): grad_stab_part + jnp.sum(d_gates.reshape(shot_count, tile_sites, gate_uni...  28.7 us
  transfers between devices with their start and end apart: 66, of which 15 were waited for; matrix products, arithmetic and copies ran while one was open for 12% of the time, Pallas kernels for 0%

commit v1 on v0

--- a/solution.py
+++ b/solution.py
@@ -228,15 +228,18 @@
     grad_weight, grad_stab_part, grad_fired, grad_keep, grad_query, grad_readout, loss_total = sums
     stab_total = lax.psum(grad_stab_part.astype(jnp.bfloat16), "rounds").astype(jnp.float32)
     totals = lax.psum(
-        (
-            grad_weight,
-            grad_fired,
-            grad_keep,
-            grad_query,
-            grad_readout * lead_tile,
-            loss_total * lead_tile,
+        lax.psum(
+            (
+                grad_weight,
+                grad_fired,
+                grad_keep,
+                grad_query,
+                grad_readout * lead_tile,
+                loss_total * lead_tile,
+            ),
+            axis_name="rounds",
         ),
-        ("rounds", "tiles"),
+        "tiles",
     )
     return (
         totals[0].reshape(3, 3, channels, gate_units),

time: 1050 us -> 988 us (0.941)
  waiting for transfers between devices: 279 us -> 232 us
  blocking collectives: 235 us -> 216 us
    psum x1, waiting for transfers between devices: 261 us -> 99.9 us  [per_device(): lax.psum((grad_weight, grad_fired, grad_keep, grad_query, grad_readout *...]
    psum x0 -> x1, waiting for transfers between devices: none -> 115 us  [per_device(): lax.psum(lax.psum((grad_weight, grad_fired, grad_keep, grad_query, grad_r...]
    psum x1, blocking collectives: 94.3 us -> 16.8 us  [per_device(): lax.psum((grad_weight, grad_fired, grad_keep, grad_query, grad_readout *...]
    psum x0 -> x1, blocking collectives: none -> 58.3 us  [per_device(): lax.psum(lax.psum((grad_weight, grad_fired, grad_keep, grad_query, grad_r...]
  transfers between devices with their start and end apart: 66 -> 67, of which waited for: 15 -> 17; matrix products, arithmetic and copies ran while one was open for 12% -> 13% of each run, Pallas kernels for 0% -> 0%
where the time goes in v1:
time: 988 us; the launch traced here: 980 us
  waiting for transfers between devices  232 us (23%)
  blocking collectives  216 us (22%)
  starting transfers between devices  189 us (19%)
  other arithmetic  167 us (17%)
  matrix products  77.6 us (8%)
  local copies, waits for them, and re-layouts  66.7 us (7%)
  loops' own time  17.1 us (2%)
  between operations  13.8 us (1%)
    psum x2, blocking collectives, one_batch(): total_exp, numer = lax.psum((part_total, part_numer), 'tiles')  141 us
    psum x1, waiting for transfers between devices, per_device(): lax.psum(lax.psum((grad_weight, grad_fired, grad_keep, grad_query, grad_r...  115 us
    psum x1, waiting for transfers between devices, per_device(): lax.psum((grad_weight, grad_fired, grad_keep, grad_query, grad_readout *...  99.9 us
    ppermute x32, starting transfers between devices, with_halo(): lax.ppermute(head, axis, [((i + 1) % count, i) for i in range(ends)])  95.2 us
    ppermute x32, starting transfers between devices, with_halo(): lax.ppermute(tail, axis, [(i, (i + 1) % count) for i in range(ends)])  93.7 us
    psum x1, blocking collectives, per_device(): lax.psum(lax.psum((grad_weight, grad_fired, grad_keep, grad_query, grad_r...  58.3 us
    dynamic_update_slice x48, other arithmetic, one_batch(): lax.scan(forward_round, initial, fired_rounds)  33.1 us
    squeeze x32, local copies, waits for them, and re-layouts, one_batch(): lax.scan(backward_round, start_back, saved, reverse=True)  29.9 us
  transfers between devices with their start and end apart: 67, of which 17 were waited for; matrix products, arithmetic and copies ran while one was open for 13% of the time, Pallas kernels for 0%

profile of v1, /device:TPU:2, one launch (start us, length us, event | category | flops | bytes accessed | tf_op | source)
XLA Modules:
  0.0 979.6 jit_solution(18416763440789632061)
XLA Ops:
  11.9 662.5 %while.108 = (s32[]{:T(128)}, f32[1152,512]{1,0:T(8,128)S(1)}, f32[128,512]{1,0:T(8,128)}, f32[512]{0:T(512)S(1)}, f32[128]{0:T(128)}, /*index=5*/f32[128]{0:T(1...) while((s32[]{:T(128)}, f32[1152,512]{1,0:T(8,128)S(1)}, ...), condition=%wide.region_15.16_spmd.clone, body=%wide.region_0.15_spmd.clone.sunk | while | flops 621755008 | bytes 24381452 | solution.py:227
  13.2 88.8 %while.109 = (s32[]{:T(128)}, bf16[1,2,64,128]{3,2,1,0:T(8,128)(2,1)S(1)}, f32[128,128]{1,0:T(8,128)S(1)}, bf16[8,1,4,66,128]{4,3,2,1,0:T(8,128)(2,1)}, f32[8,12...) while((s32[]{:T(128)}, ...), condition=%wide.region_2.2_spmd.clone, body=%wide.region_1.1_spmd.clone.sunk | while | flops 152739968 | bytes 4702967 | solution.py:169
  15.2 2.4 collective-permute-start.1
  18.4 2.5 collective-permute-done.1
  26.8 2.4 collective-permute-start.1
  37.8 2.4 collective-permute-start.1
  48.8 2.4 collective-permute-start.1
  59.9 2.4 collective-permute-start.1
  70.9 2.4 collective-permute-start.1
  81.9 2.4 collective-permute-start.1
  92.9 2.4 collective-permute-start.1
  103.6 68.7 %all-reduce.6 = (f32[]{:T(128)}, f32[1,128]{1,0:T(1,128)S(1)}) all-reduce(f32[]{:T(128)} %get-tuple-element.1444, f32[1,128]{1,0:T(1,128)S(1)} %bitcast.186), channel_id=1, replica_groups=mesh['rounds'=8,'tiles'=32] {'tiles'}, use_global_device_ids=true, to_apply=%region_5.5 | all-reduce | flops 129 | bytes 1032 | tf_op jit(solution)/shard_map/while/body/eval_jaxpr/psum | solution.py:175
  172.3 2.0 fusion.110
  186.5 148.4 %while.110 = (s32[]{:T(128)}, f32[128,128]{1,0:T(8,128)S(1)}, f32[128,128]{1,0:T(8,128)}, f32[1152,512]{1,0:T(8,128)S(1)}, f32[128,512]{1,0:T(8,128)}, /*index=5...) while((s32[]{:T(128)}, f32[128,128]{1,0:T(8,128)S(1)}, ...), condition=%wide.region_13.13_spmd.clone, body=%wide.region_11.12_spmd.clone.sunk | while | flops 468750976 | bytes 19420224 | solution.py:203
  190.4 6.0 collective-permute-start.2
  211.0 3.6 collective-permute-start.2
  229.3 3.6 collective-permute-start.2
  247.6 3.6 collective-permute-start.2
  265.8 3.6 collective-permute-start.2
  284.0 3.6 collective-permute-start.2
  302.3 3.6 collective-permute-start.2
  320.6 3.6 collective-permute-start.2
  336.3 100.8 %while.109 = (s32[]{:T(128)}, bf16[1,2,64,128]{3,2,1,0:T(8,128)(2,1)S(1)}, f32[128,128]{1,0:T(8,128)S(1)}, bf16[8,1,4,66,128]{4,3,2,1,0:T(8,128)(2,1)}, f32[8,12...) while((s32[]{:T(128)}, ...), condition=%wide.region_2.2_spmd.clone, body=%wide.region_1.1_spmd.clone.sunk | while | flops 152739968 | bytes 4702967 | solution.py:169
  336.3 3.6 collective-permute-start
  340.0 3.2 collective-permute-start.1
  351.0 4.8 collective-permute-start.1
  362.5 5.7 collective-permute-start.1
  375.1 5.8 collective-permute-start.1
  387.7 5.7 collective-permute-start.1
  400.2 5.8 collective-permute-start.1
  412.8 6.4 collective-permute-start.1
  425.9 6.3 collective-permute-start.1
  438.7 72.4 %all-reduce.6 = (f32[]{:T(128)}, f32[1,128]{1,0:T(1,128)S(1)}) all-reduce(f32[]{:T(128)} %get-tuple-element.1444, f32[1,128]{1,0:T(1,128)S(1)} %bitcast.186), channel_id=1, replica_groups=mesh['rounds'=8,'tiles'=32] {'tiles'}, use_global_device_ids=true, to_apply=%region_5.5 | all-reduce | flops 129 | bytes 1032 | tf_op jit(solution)/shard_map/while/body/eval_jaxpr/psum | solution.py:175
  511.0 2.0 fusion.110
  525.9 148.4 %while.110 = (s32[]{:T(128)}, f32[128,128]{1,0:T(8,128)S(1)}, f32[128,128]{1,0:T(8,128)}, f32[1152,512]{1,0:T(8,128)S(1)}, f32[128,512]{1,0:T(8,128)}, /*index=5...) while((s32[]{:T(128)}, f32[128,128]{1,0:T(8,128)S(1)}, ...), condition=%wide.region_13.13_spmd.clone, body=%wide.region_11.12_spmd.clone.sunk | while | flops 468750976 | bytes 19420224 | solution.py:203
  529.8 6.0 collective-permute-start.2
  550.4 3.6 collective-permute-start.2
  568.6 3.6 collective-permute-start.2
  586.9 3.6 collective-permute-start.2
  605.2 3.6 collective-permute-start.2
  623.4 3.6 collective-permute-start.2
  641.7 3.6 collective-permute-start.2
  660.0 3.6 collective-permute-start.2
  677.5 99.9 %all-reduce.11.cloned.1.call-done = f32[1152,512]{1,0:T(8,128)} async-done(((f32[1152,512]{1,0:T(8,128)}), f32[1152,512]{1,0:T(8,128)}) %all-reduce.11.cloned.1.call-update) | async-done | bytes 2359312 | tf_op jit(solution)/shard_map/psum | solution.py:231
  778.1 16.8 %all-reduce.4 = (f32[512]{0:T(512)S(1)}, f32[128]{0:T(128)S(1)}, f32[128]{0:T(128)S(1)}, f32[128]{0:T(128)S(1)}, f32[]{:T(128)}) all-reduce(f32[512]{0:T(512)S(1)} %get-tuple-element.1697, f32[128]{0:T(128)S(1)} %copy-done.13, f32[128]{0:T(128)} %get-tuple-element.1699, ...), channel_id=1, replica_groups=mesh['rounds'=8,'tiles'=32] {'rounds'}, use_global_device_ids=true, to_apply=%region_19.20 | all-reduce | flops 897 | bytes 7176 | tf_op jit(solution)/shard_map/psum | solution.py:231
  794.9 58.3 %all-reduce.3 = (f32[512]{0:T(512)}, f32[128]{0:T(128)}, f32[128]{0:T(128)}, f32[128]{0:T(128)}, f32[]{:T(128)}) all-reduce(f32[512]{0:T(512)S(1)} %get-tuple-element.1095, f32[128]{0:T(128)S(1)} %get-tuple-element.1096, f32[128]{0:T(128)S(1)} %get-tuple-element.1097, ...), channel_id=1, replica_groups=mesh['rounds'=8,'tiles'=32] {'tiles'}, use_global_device_ids=true, to_apply=%region_20.21 | all-reduce | flops 897 | bytes 7176 | tf_op jit(solution)/shard_map/psum | solution.py:230
  854.9 114.9 %all-reduce.13.cloned.1.call-done = f32[3,3,128,512]{3,2,1,0:T(8,128)} async-done(((f32[3,3,128,512]{3,2,1,0:T(8,128)}), f32[3,3,128,512]{3,2,1,0:T(8,128)}) %all-reduce.13.cloned.1.call-update) | async-done | bytes 2359312 | tf_op jit(solution)/shard_map/psum | solution.py:230
  969.8 3.3 copy.109
  (1190 shorter events, 378.6 us)
Async XLA Ops:
  7.2 770.2 %all-reduce.11.cloned.1.call-start = ((), (), s32[]{:S(2)}) async-start(), calls=%async_computation | async-start | bytes 4718592 | tf_op jit(solution)/shard_map/psum | solution.py:231
  190.4 15.2 %collective-permute-start.2 = (bf16[1,1,64,512]{3,2,1,0:T(8,128)(2,1)}, bf16[1,1,64,512]{3,2,1,0:T(8,128)(2,1)}, u32[]{:S(2)}, u32[]{:S(2)}) collective-permute-start(bf16[1,1,64,512]{3,2,1,0:T(8,128)(2,1)} %get-tuple-element.1499), channel_id=1, source_target_pairs={{1,0},{2,1},{3,2},{4,3},{5,4},{6,5},{7,6},{8,7},{9,8},{10,9},{11,1... | collective-permute-start | bytes 196616 | tf_op jit(solution)/shard_map/while/body/eval_jaxpr/while/body/eval_jaxpr/ppermute | solution.py:18
  196.4 9.2 collective-permute-start.3
  211.0 12.8 %collective-permute-start.2 = (bf16[1,1,64,512]{3,2,1,0:T(8,128)(2,1)}, bf16[1,1,64,512]{3,2,1,0:T(8,128)(2,1)}, u32[]{:S(2)}, u32[]{:S(2)}) collective-permute-start(bf16[1,1,64,512]{3,2,1,0:T(8,128)(2,1)} %get-tuple-element.1499), channel_id=1, source_target_pairs={{1,0},{2,1},{3,2},{4,3},{5,4},{6,5},{7,6},{8,7},{9,8},{10,9},{11,1... | collective-permute-start | bytes 196616 | tf_op jit(solution)/shard_map/while/body/eval_jaxpr/while/body/eval_jaxpr/ppermute | solution.py:18
  214.7 9.2 collective-permute-start.3
  229.3 12.9 %collective-permute-start.2 = (bf16[1,1,64,512]{3,2,1,0:T(8,128)(2,1)}, bf16[1,1,64,512]{3,2,1,0:T(8,128)(2,1)}, u32[]{:S(2)}, u32[]{:S(2)}) collective-permute-start(bf16[1,1,64,512]{3,2,1,0:T(8,128)(2,1)} %get-tuple-element.1499), channel_id=1, source_target_pairs={{1,0},{2,1},{3,2},{4,3},{5,4},{6,5},{7,6},{8,7},{9,8},{10,9},{11,1... | collective-permute-start | bytes 196616 | tf_op jit(solution)/shard_map/while/body/eval_jaxpr/while/body/eval_jaxpr/ppermute | solution.py:18
  232.9 9.2 collective-permute-start.3
  247.6 12.8 %collective-permute-start.2 = (bf16[1,1,64,512]{3,2,1,0:T(8,128)(2,1)}, bf16[1,1,64,512]{3,2,1,0:T(8,128)(2,1)}, u32[]{:S(2)}, u32[]{:S(2)}) collective-permute-start(bf16[1,1,64,512]{3,2,1,0:T(8,128)(2,1)} %get-tuple-element.1499), channel_id=1, source_target_pairs={{1,0},{2,1},{3,2},{4,3},{5,4},{6,5},{7,6},{8,7},{9,8},{10,9},{11,1... | collective-permute-start | bytes 196616 | tf_op jit(solution)/shard_map/while/body/eval_jaxpr/while/body/eval_jaxpr/ppermute | solution.py:18
  251.2 9.2 collective-permute-start.3
  265.8 12.8 %collective-permute-start.2 = (bf16[1,1,64,512]{3,2,1,0:T(8,128)(2,1)}, bf16[1,1,64,512]{3,2,1,0:T(8,128)(2,1)}, u32[]{:S(2)}, u32[]{:S(2)}) collective-permute-start(bf16[1,1,64,512]{3,2,1,0:T(8,128)(2,1)} %get-tuple-element.1499), channel_id=1, source_target_pairs={{1,0},{2,1},{3,2},{4,3},{5,4},{6,5},{7,6},{8,7},{9,8},{10,9},{11,1... | collective-permute-start | bytes 196616 | tf_op jit(solution)/shard_map/while/body/eval_jaxpr/while/body/eval_jaxpr/ppermute | solution.py:18
  269.5 9.2 collective-permute-start.3
  284.0 12.8 %collective-permute-start.2 = (bf16[1,1,64,512]{3,2,1,0:T(8,128)(2,1)}, bf16[1,1,64,512]{3,2,1,0:T(8,128)(2,1)}, u32[]{:S(2)}, u32[]{:S(2)}) collective-permute-start(bf16[1,1,64,512]{3,2,1,0:T(8,128)(2,1)} %get-tuple-element.1499), channel_id=1, source_target_pairs={{1,0},{2,1},{3,2},{4,3},{5,4},{6,5},{7,6},{8,7},{9,8},{10,9},{11,1... | collective-permute-start | bytes 196616 | tf_op jit(solution)/shard_map/while/body/eval_jaxpr/while/body/eval_jaxpr/ppermute | solution.py:18
  287.7 9.2 collective-permute-start.3
  302.3 12.8 %collective-permute-start.2 = (bf16[1,1,64,512]{3,2,1,0:T(8,128)(2,1)}, bf16[1,1,64,512]{3,2,1,0:T(8,128)(2,1)}, u32[]{:S(2)}, u32[]{:S(2)}) collective-permute-start(bf16[1,1,64,512]{3,2,1,0:T(8,128)(2,1)} %get-tuple-element.1499), channel_id=1, source_target_pairs={{1,0},{2,1},{3,2},{4,3},{5,4},{6,5},{7,6},{8,7},{9,8},{10,9},{11,1... | collective-permute-start | bytes 196616 | tf_op jit(solution)/shard_map/while/body/eval_jaxpr/while/body/eval_jaxpr/ppermute | solution.py:18
  305.9 9.2 collective-permute-start.3
  320.6 12.9 %collective-permute-start.2 = (bf16[1,1,64,512]{3,2,1,0:T(8,128)(2,1)}, bf16[1,1,64,512]{3,2,1,0:T(8,128)(2,1)}, u32[]{:S(2)}, u32[]{:S(2)}) collective-permute-start(bf16[1,1,64,512]{3,2,1,0:T(8,128)(2,1)} %get-tuple-element.1499), channel_id=1, source_target_pairs={{1,0},{2,1},{3,2},{4,3},{5,4},{6,5},{7,6},{8,7},{9,8},{10,9},{11,1... | collective-permute-start | bytes 196616 | tf_op jit(solution)/shard_map/while/body/eval_jaxpr/while/body/eval_jaxpr/ppermute | solution.py:18
  324.2 9.2 collective-permute-start.3
  336.3 7.6 collective-permute-start
  349.1 7.4 collective-permute-start
  360.6 8.4 collective-permute-start
  362.5 6.6 collective-permute-start.1
  373.2 8.4 collective-permute-start
  375.1 6.6 collective-permute-start.1
  385.8 8.4 collective-permute-start
  398.3 8.5 collective-permute-start
  400.2 6.6 collective-permute-start.1
  410.8 9.0 collective-permute-start
  412.8 7.2 collective-permute-start.1
  424.0 9.0 collective-permute-start
  425.9 7.1 collective-permute-start.1
  529.8 15.2 %collective-permute-start.2 = (bf16[1,1,64,512]{3,2,1,0:T(8,128)(2,1)}, bf16[1,1,64,512]{3,2,1,0:T(8,128)(2,1)}, u32[]{:S(2)}, u32[]{:S(2)}) collective-permute-start(bf16[1,1,64,512]{3,2,1,0:T(8,128)(2,1)} %get-tuple-element.1499), channel_id=1, source_target_pairs={{1,0},{2,1},{3,2},{4,3},{5,4},{6,5},{7,6},{8,7},{9,8},{10,9},{11,1... | collective-permute-start | bytes 196616 | tf_op jit(solution)/shard_map/while/body/eval_jaxpr/while/body/eval_jaxpr/ppermute | solution.py:18
  535.8 9.2 collective-permute-start.3
  550.4 12.8 %collective-permute-start.2 = (bf16[1,1,64,512]{3,2,1,0:T(8,128)(2,1)}, bf16[1,1,64,512]{3,2,1,0:T(8,128)(2,1)}, u32[]{:S(2)}, u32[]{:S(2)}) collective-permute-start(bf16[1,1,64,512]{3,2,1,0:T(8,128)(2,1)} %get-tuple-element.1499), channel_id=1, source_target_pairs={{1,0},{2,1},{3,2},{4,3},{5,4},{6,5},{7,6},{8,7},{9,8},{10,9},{11,1... | collective-permute-start | bytes 196616 | tf_op jit(solution)/shard_map/while/body/eval_jaxpr/while/body/eval_jaxpr/ppermute | solution.py:18
  554.1 9.2 collective-permute-start.3
  568.6 12.9 %collective-permute-start.2 = (bf16[1,1,64,512]{3,2,1,0:T(8,128)(2,1)}, bf16[1,1,64,512]{3,2,1,0:T(8,128)(2,1)}, u32[]{:S(2)}, u32[]{:S(2)}) collective-permute-start(bf16[1,1,64,512]{3,2,1,0:T(8,128)(2,1)} %get-tuple-element.1499), channel_id=1, source_target_pairs={{1,0},{2,1},{3,2},{4,3},{5,4},{6,5},{7,6},{8,7},{9,8},{10,9},{11,1... | collective-permute-start | bytes 196616 | tf_op jit(solution)/shard_map/while/body/eval_jaxpr/while/body/eval_jaxpr/ppermute | solution.py:18
  572.3 9.2 collective-permute-start.3
  586.9 12.8 %collective-permute-start.2 = (bf16[1,1,64,512]{3,2,1,0:T(8,128)(2,1)}, bf16[1,1,64,512]{3,2,1,0:T(8,128)(2,1)}, u32[]{:S(2)}, u32[]{:S(2)}) collective-permute-start(bf16[1,1,64,512]{3,2,1,0:T(8,128)(2,1)} %get-tuple-element.1499), channel_id=1, source_target_pairs={{1,0},{2,1},{3,2},{4,3},{5,4},{6,5},{7,6},{8,7},{9,8},{10,9},{11,1... | collective-permute-start | bytes 196616 | tf_op jit(solution)/shard_map/while/body/eval_jaxpr/while/body/eval_jaxpr/ppermute | solution.py:18
  590.6 9.2 collective-permute-start.3
  605.2 12.8 %collective-permute-start.2 = (bf16[1,1,64,512]{3,2,1,0:T(8,128)(2,1)}, bf16[1,1,64,512]{3,2,1,0:T(8,128)(2,1)}, u32[]{:S(2)}, u32[]{:S(2)}) collective-permute-start(bf16[1,1,64,512]{3,2,1,0:T(8,128)(2,1)} %get-tuple-element.1499), channel_id=1, source_target_pairs={{1,0},{2,1},{3,2},{4,3},{5,4},{6,5},{7,6},{8,7},{9,8},{10,9},{11,1... | collective-permute-start | bytes 196616 | tf_op jit(solution)/shard_map/while/body/eval_jaxpr/while/body/eval_jaxpr/ppermute | solution.py:18
  608.8 9.2 collective-permute-start.3
  623.4 12.8 %collective-permute-start.2 = (bf16[1,1,64,512]{3,2,1,0:T(8,128)(2,1)}, bf16[1,1,64,512]{3,2,1,0:T(8,128)(2,1)}, u32[]{:S(2)}, u32[]{:S(2)}) collective-permute-start(bf16[1,1,64,512]{3,2,1,0:T(8,128)(2,1)} %get-tuple-element.1499), channel_id=1, source_target_pairs={{1,0},{2,1},{3,2},{4,3},{5,4},{6,5},{7,6},{8,7},{9,8},{10,9},{11,1... | collective-permute-start | bytes 196616 | tf_op jit(solution)/shard_map/while/body/eval_jaxpr/while/body/eval_jaxpr/ppermute | solution.py:18
  627.1 9.2 collective-permute-start.3
  641.7 12.8 %collective-permute-start.2 = (bf16[1,1,64,512]{3,2,1,0:T(8,128)(2,1)}, bf16[1,1,64,512]{3,2,1,0:T(8,128)(2,1)}, u32[]{:S(2)}, u32[]{:S(2)}) collective-permute-start(bf16[1,1,64,512]{3,2,1,0:T(8,128)(2,1)} %get-tuple-element.1499), channel_id=1, source_target_pairs={{1,0},{2,1},{3,2},{4,3},{5,4},{6,5},{7,6},{8,7},{9,8},{10,9},{11,1... | collective-permute-start | bytes 196616 | tf_op jit(solution)/shard_map/while/body/eval_jaxpr/while/body/eval_jaxpr/ppermute | solution.py:18
  645.3 9.2 collective-permute-start.3
  660.0 12.9 %collective-permute-start.2 = (bf16[1,1,64,512]{3,2,1,0:T(8,128)(2,1)}, bf16[1,1,64,512]{3,2,1,0:T(8,128)(2,1)}, u32[]{:S(2)}, u32[]{:S(2)}) collective-permute-start(bf16[1,1,64,512]{3,2,1,0:T(8,128)(2,1)} %get-tuple-element.1499), channel_id=1, source_target_pairs={{1,0},{2,1},{3,2},{4,3},{5,4},{6,5},{7,6},{8,7},{9,8},{10,9},{11,1... | collective-permute-start | bytes 196616 | tf_op jit(solution)/shard_map/while/body/eval_jaxpr/while/body/eval_jaxpr/ppermute | solution.py:18
  663.6 9.2 collective-permute-start.3
  675.8 177.5 %all-reduce.15.cloned.1.call-start = ((), (), s32[]{:S(2)}) async-start(), calls=%async_computation.2 | async-start | bytes 262144 | tf_op jit(solution)/shard_map/psum | solution.py:229
  677.5 292.3 %all-reduce.13.cloned.1.call-start = ((), (), s32[]{:S(2)}) async-start(), calls=%async_computation.1 | async-start | bytes 4718592 | tf_op jit(solution)/shard_map/psum | solution.py:230
  (199 other events, 1039.4 us)
Sparse Core Ops, SparseCore 0:
  675.9 101.4 all-reduce.10
  779.7 71.1 all-reduce.14
  854.3 115.4 all-reduce.12
